TPU v7x, 512 devices: a whole 4x4x16 slice. The times are simulated.
512 devices in a mesh: blk: 32 (over z_lo, y), head: 8 (over x, z_hi), batch: 2 (over core).
Axes of the slice: x: 4, y: 4, z: 16 (z_hi: 2, z_lo: 8; z = z_hi * 8 + z_lo), core: 2. Of those that a mesh axis runs over, the one named last changes fastest.
Arguments:
- query_rows: bfloat16 [16384, 3072], P(('batch', 'blk', 'head')), parts along dimension 0, may hold values from -16 to 16
- key_rows: bfloat16 [16384, 3072], P(('batch', 'blk', 'head')), parts along dimension 0, may hold values from -16 to 16
- value_rows: bfloat16 [16384, 3072], P(('batch', 'blk', 'head')), parts along dimension 0, may hold values from -6 to 6
- q_gain: float32 [3072], replicated, may hold values from 1 to 3
- k_gain: float32 [3072], replicated, may hold values from 1 to 3
- tile_mask: int32 [64, 64], replicated, may hold values from 0 to 1, as said below
Outputs:
- attended: bfloat16 [16384, 3072], P(('batch', 'blk', 'head')), parts along dimension 0
There are 2 independent parts, one for each index of `batch`. A program takes and returns all parts, laid end to end along the dimension named above; an argument that names none is the same for every part. Nothing has to cross between parts.
Inputs may be any that keep to these rules, and one draw needn't show every extreme that they name: `tile_mask`: 1 where a block of 128 query positions may attend to a block of 128 key positions; the main diagonal and the two beside it are always 1.
All inputs are finite; a program needn't handle non-finite values.
Results may differ from a plain program's by a relative error of at most 0.012.
The roundings to bfloat16 on the way count: a program that leaves them out, or rounds other values in their place, can miss the bound.
Values may be sent and summed in bfloat16 or wider, within the bound.
A program may use at most 128 MiB of HBM per device.

v0:
```python
import jax
import jax.numpy as jnp
from jax import lax
from jax.sharding import PartitionSpec as P

HEADS = 24
HDIM = 128
TILE = 128


def shifted(block, axis, distance):
    devices = range(lax.axis_size(axis))
    route = [((i - distance) % len(devices), i) for i in devices]
    return lax.ppermute(block, axis, route)


def normalize(inputs, weights):
    widened = inputs.astype(jnp.float32)
    mean_square = jnp.mean(widened * widened, axis=-1, keepdims=True)
    return (widened * lax.rsqrt(mean_square + 1e-06) * weights).astype(jnp.bfloat16)


def per_device(query_rows, key_rows, value_rows, q_gain, k_gain, tile_mask):
    row_count = query_rows.shape[0]
    shaped = (row_count, HEADS, HDIM)
    q_local = normalize(query_rows, q_gain).reshape(shaped)
    k_local = normalize(key_rows, k_gain).reshape(shaped)
    v_local = value_rows.reshape(shaped)
    q_heads, k_heads, v_heads = (
        lax.all_to_all(q_local, "head", split_axis=1, concat_axis=0, tiled=True),
        lax.all_to_all(k_local, "head", split_axis=1, concat_axis=0, tiled=True),
        lax.all_to_all(v_local, "head", split_axis=1, concat_axis=0, tiled=True),
    )
    q_count = q_heads.shape[0]
    local_heads = q_heads.shape[1]
    cycle_size = lax.axis_size("blk")
    position = lax.axis_index("blk")
    tiles_here = q_count // TILE
    mask_rows = lax.dynamic_slice_in_dim(tile_mask, position * tiles_here, tiles_here, 0) != 0
    allowed_all = jnp.repeat(jnp.repeat(mask_rows, TILE, axis=0), TILE, axis=1)
    kv_pair = jnp.stack([k_heads, v_heads])
    score_scale = HDIM ** (-0.5)

    def absorb(state_now, kv_piece, first_row):
        allowed = lax.dynamic_slice_in_dim(allowed_all, first_row, kv_piece.shape[1], 1)

        def attend(state_in):
            running_max, totals, weighted = state_in
            scores = (
                jnp.einsum("qhd,khd->hqk", q_heads, kv_piece[0], preferred_element_type=jnp.float32)
                * score_scale
            )
            scores = jnp.where(allowed[None], scores, -1e30)
            new_max = jnp.maximum(running_max, jnp.max(scores, axis=-1))
            weights = jnp.where(allowed[None], jnp.exp(scores - new_max[:, :, None]), 0.0)
            rescale = jnp.exp(running_max - new_max)
            totals = totals * rescale + jnp.sum(weights, axis=-1)
            product = jnp.einsum(
                "hqk,khd->qhd",
                weights.astype(jnp.bfloat16),
                kv_piece[1],
                preferred_element_type=jnp.float32,
            )
            weighted = weighted * jnp.transpose(rescale)[:, :, None] + product
            return (new_max, totals, weighted)

        def keep_state(state_in):
            return state_in

        return lax.cond(jnp.any(allowed), attend, keep_state, state_now)

    start_state = (
        jnp.full((local_heads, q_count), -1e30, jnp.float32),
        jnp.zeros((local_heads, q_count), jnp.float32),
        jnp.zeros((q_count, local_heads, HDIM), jnp.float32),
    )
    own_state = absorb(start_state, kv_pair, position * q_count)

    def cycle_turn(step, loop_state):
        state_in, kv_now = loop_state
        kv_next = shifted(kv_now, "blk", 1)
        source = (position - step) % cycle_size
        return (absorb(state_in, kv_next, source * q_count), kv_next)

    final_state, unused_pair = lax.fori_loop(1, cycle_size, cycle_turn, (own_state, kv_pair))
    running_max, totals, weighted = final_state
    mixed = (weighted / jnp.transpose(totals)[:, :, None]).astype(jnp.bfloat16)
    returned = lax.all_to_all(mixed, "head", split_axis=0, concat_axis=1, tiled=True)
    return returned.reshape(row_count, HEADS * HDIM)


def solution(mesh):
    return jax.shard_map(
        per_device,
        mesh=mesh,
        in_specs=(
            P(("batch", "blk", "head"), None),
            P(("batch", "blk", "head"), None),
            P(("batch", "blk", "head"), None),
            P(),
            P(),
            P(),
        ),
        out_specs=P(("batch", "blk", "head"), None),
        check_vma=False,
    )
```

profile of v0, /device:TPU:6, one launch (start us, length us, event | category | flops | bytes accessed | tf_op | source)
XLA Modules:
  0.0 753.8 jit_solution(3310050864245813316)
XLA Ops:
  2.9 18.0 %all-to-all-start.1 = ((bf16[32,24,128]{2,0,1:T(8,128)(2,1)}), bf16[32,24,128]{2,0,1:T(8,128)(2,1)S(1)}, u32[]{:S(2)}, u32[]{:S(2)}) async-start(bf16[32,24,128]{2,0,1:T(8,128)(2,1)} %copy_bitcast_fusion.2), calls=%async_computation.1 | async-start | bytes 393216 | tf_op jit(solution)/shard_map/all_to_all | solution.py:30
  23.7 12.1 %all-to-all-done.1 = bf16[32,24,128]{2,0,1:T(8,128)(2,1)S(1)} async-done(((bf16[32,24,128]{2,0,1:T(8,128)(2,1)}), bf16[32,24,128]{2,0,1:T(8,128)(2,1)S(1)}, u32[]{:S(2)}, u32[]{:S(2)}) %all-to-all-start.1) | async-done | bytes 196640 | tf_op jit(solution)/shard_map/all_to_all | solution.py:30
  35.8 4.5 all-to-all-start
  41.1 15.3 %all-to-all-done = bf16[32,24,128]{2,0,1:T(8,128)(2,1)S(1)} async-done(((bf16[32,24,128]{2,0,1:T(8,128)(2,1)}), bf16[32,24,128]{2,0,1:T(8,128)(2,1)S(1)}, u32[]{:S(2)}, u32[]{:S(2)}) %all-to-all-start) | async-done | bytes 196640 | tf_op jit(solution)/shard_map/all_to_all | solution.py:31
  56.3 4.5 all-to-all-start.2
  63.8 12.6 %all-to-all-done.2 = bf16[32,24,128]{2,0,1:T(8,128)(2,1)S(1)} async-done(((bf16[32,24,128]{2,0,1:T(8,128)(2,1)}), bf16[32,24,128]{2,0,1:T(8,128)(2,1)S(1)}, u32[]{:S(2)}, u32[]{:S(2)}) %all-to-all-start.2) | async-done | bytes 196640 | tf_op jit(solution)/shard_map/all_to_all | solution.py:32
  77.1 3.6 conditional.2
  80.7 653.7 %while.21 = (s32[]{:T(128)}, f32[3,256]{1,0:T(4,128)}, f32[3,256]{1,0:T(4,128)S(1)}, f32[256,3,128]{2,0,1:T(8,128)S(1)}, bf16[2,256,3,128]{3,1,2,0:T(8,128)(2,1)...) while((s32[]{:T(128)}, f32[3,256]{1,0:T(4,128)}, ...), condition=%wide.region_13.14_spmd, body=%wide.region_7.13_spmd.sunk | while | flops 102697232 | bytes 6474182 | solution.py:85
  80.7 3.5 collective-permute-start
  85.5 13.8 %collective-permute-done = bf16[2,256,3,128]{3,1,2,0:T(8,128)(2,1)S(1)} collective-permute-done((bf16[2,256,3,128]{3,1,2,0:T(8,128)(2,1)}, bf16[2,256,3,128]{3,1,2,0:T(8,128)(2,1)S(1)}, u32[]{:S(2)}, u32[]{:S(2)}) %collective-permute-start) | collective-permute-done | bytes 393248 | tf_op jit(solution)/shard_map/while/body/eval_jaxpr/ppermute | solution.py:14
  100.1 1.9 collective-permute-start
  103.3 15.4 %collective-permute-done = bf16[2,256,3,128]{3,1,2,0:T(8,128)(2,1)S(1)} collective-permute-done((bf16[2,256,3,128]{3,1,2,0:T(8,128)(2,1)}, bf16[2,256,3,128]{3,1,2,0:T(8,128)(2,1)S(1)}, u32[]{:S(2)}, u32[]{:S(2)}) %collective-permute-start) | collective-permute-done | bytes 393248 | tf_op jit(solution)/shard_map/while/body/eval_jaxpr/ppermute | solution.py:14
  122.6 15.4 %collective-permute-done = bf16[2,256,3,128]{3,1,2,0:T(8,128)(2,1)S(1)} collective-permute-done((bf16[2,256,3,128]{3,1,2,0:T(8,128)(2,1)}, bf16[2,256,3,128]{3,1,2,0:T(8,128)(2,1)S(1)}, u32[]{:S(2)}, u32[]{:S(2)}) %collective-permute-start) | collective-permute-done | bytes 393248 | tf_op jit(solution)/shard_map/while/body/eval_jaxpr/ppermute | solution.py:14
  138.0 2.9 conditional.4
  144.8 15.4 %collective-permute-done = bf16[2,256,3,128]{3,1,2,0:T(8,128)(2,1)S(1)} collective-permute-done((bf16[2,256,3,128]{3,1,2,0:T(8,128)(2,1)}, bf16[2,256,3,128]{3,1,2,0:T(8,128)(2,1)S(1)}, u32[]{:S(2)}, u32[]{:S(2)}) %collective-permute-start) | collective-permute-done | bytes 393248 | tf_op jit(solution)/shard_map/while/body/eval_jaxpr/ppermute | solution.py:14
  164.2 15.4 %collective-permute-done = bf16[2,256,3,128]{3,1,2,0:T(8,128)(2,1)S(1)} collective-permute-done((bf16[2,256,3,128]{3,1,2,0:T(8,128)(2,1)}, bf16[2,256,3,128]{3,1,2,0:T(8,128)(2,1)S(1)}, u32[]{:S(2)}, u32[]{:S(2)}) %collective-permute-start) | collective-permute-done | bytes 393248 | tf_op jit(solution)/shard_map/while/body/eval_jaxpr/ppermute | solution.py:14
  179.5 2.9 conditional.4
  186.4 15.7 %collective-permute-done = bf16[2,256,3,128]{3,1,2,0:T(8,128)(2,1)S(1)} collective-permute-done((bf16[2,256,3,128]{3,1,2,0:T(8,128)(2,1)}, bf16[2,256,3,128]{3,1,2,0:T(8,128)(2,1)S(1)}, u32[]{:S(2)}, u32[]{:S(2)}) %collective-permute-start) | collective-permute-done | bytes 393248 | tf_op jit(solution)/shard_map/while/body/eval_jaxpr/ppermute | solution.py:14
  206.1 16.9 %collective-permute-done = bf16[2,256,3,128]{3,1,2,0:T(8,128)(2,1)S(1)} collective-permute-done((bf16[2,256,3,128]{3,1,2,0:T(8,128)(2,1)}, bf16[2,256,3,128]{3,1,2,0:T(8,128)(2,1)S(1)}, u32[]{:S(2)}, u32[]{:S(2)}) %collective-permute-start) | collective-permute-done | bytes 393248 | tf_op jit(solution)/shard_map/while/body/eval_jaxpr/ppermute | solution.py:14
  227.0 18.0 %collective-permute-done = bf16[2,256,3,128]{3,1,2,0:T(8,128)(2,1)S(1)} collective-permute-done((bf16[2,256,3,128]{3,1,2,0:T(8,128)(2,1)}, bf16[2,256,3,128]{3,1,2,0:T(8,128)(2,1)S(1)}, u32[]{:S(2)}, u32[]{:S(2)}) %collective-permute-start) | collective-permute-done | bytes 393248 | tf_op jit(solution)/shard_map/while/body/eval_jaxpr/ppermute | solution.py:14
  249.0 19.2 %collective-permute-done = bf16[2,256,3,128]{3,1,2,0:T(8,128)(2,1)S(1)} collective-permute-done((bf16[2,256,3,128]{3,1,2,0:T(8,128)(2,1)}, bf16[2,256,3,128]{3,1,2,0:T(8,128)(2,1)S(1)}, u32[]{:S(2)}, u32[]{:S(2)}) %collective-permute-start) | collective-permute-done | bytes 393248 | tf_op jit(solution)/shard_map/while/body/eval_jaxpr/ppermute | solution.py:14
  272.1 18.8 %collective-permute-done = bf16[2,256,3,128]{3,1,2,0:T(8,128)(2,1)S(1)} collective-permute-done((bf16[2,256,3,128]{3,1,2,0:T(8,128)(2,1)}, bf16[2,256,3,128]{3,1,2,0:T(8,128)(2,1)S(1)}, u32[]{:S(2)}, u32[]{:S(2)}) %collective-permute-start) | collective-permute-done | bytes 393248 | tf_op jit(solution)/shard_map/while/body/eval_jaxpr/ppermute | solution.py:14
  294.9 17.9 %collective-permute-done = bf16[2,256,3,128]{3,1,2,0:T(8,128)(2,1)S(1)} collective-permute-done((bf16[2,256,3,128]{3,1,2,0:T(8,128)(2,1)}, bf16[2,256,3,128]{3,1,2,0:T(8,128)(2,1)S(1)}, u32[]{:S(2)}, u32[]{:S(2)}) %collective-permute-start) | collective-permute-done | bytes 393248 | tf_op jit(solution)/shard_map/while/body/eval_jaxpr/ppermute | solution.py:14
  316.8 17.1 %collective-permute-done = bf16[2,256,3,128]{3,1,2,0:T(8,128)(2,1)S(1)} collective-permute-done((bf16[2,256,3,128]{3,1,2,0:T(8,128)(2,1)}, bf16[2,256,3,128]{3,1,2,0:T(8,128)(2,1)S(1)}, u32[]{:S(2)}, u32[]{:S(2)}) %collective-permute-start) | collective-permute-done | bytes 393248 | tf_op jit(solution)/shard_map/while/body/eval_jaxpr/ppermute | solution.py:14
  337.9 16.2 %collective-permute-done = bf16[2,256,3,128]{3,1,2,0:T(8,128)(2,1)S(1)} collective-permute-done((bf16[2,256,3,128]{3,1,2,0:T(8,128)(2,1)}, bf16[2,256,3,128]{3,1,2,0:T(8,128)(2,1)S(1)}, u32[]{:S(2)}, u32[]{:S(2)}) %collective-permute-start) | collective-permute-done | bytes 393248 | tf_op jit(solution)/shard_map/while/body/eval_jaxpr/ppermute | solution.py:14
  358.1 15.4 %collective-permute-done = bf16[2,256,3,128]{3,1,2,0:T(8,128)(2,1)S(1)} collective-permute-done((bf16[2,256,3,128]{3,1,2,0:T(8,128)(2,1)}, bf16[2,256,3,128]{3,1,2,0:T(8,128)(2,1)S(1)}, u32[]{:S(2)}, u32[]{:S(2)}) %collective-permute-start) | collective-permute-done | bytes 393248 | tf_op jit(solution)/shard_map/while/body/eval_jaxpr/ppermute | solution.py:14
  377.4 15.4 %collective-permute-done = bf16[2,256,3,128]{3,1,2,0:T(8,128)(2,1)S(1)} collective-permute-done((bf16[2,256,3,128]{3,1,2,0:T(8,128)(2,1)}, bf16[2,256,3,128]{3,1,2,0:T(8,128)(2,1)S(1)}, u32[]{:S(2)}, u32[]{:S(2)}) %collective-permute-start) | collective-permute-done | bytes 393248 | tf_op jit(solution)/shard_map/while/body/eval_jaxpr/ppermute | solution.py:14
  396.7 16.3 %collective-permute-done = bf16[2,256,3,128]{3,1,2,0:T(8,128)(2,1)S(1)} collective-permute-done((bf16[2,256,3,128]{3,1,2,0:T(8,128)(2,1)}, bf16[2,256,3,128]{3,1,2,0:T(8,128)(2,1)S(1)}, u32[]{:S(2)}, u32[]{:S(2)}) %collective-permute-start) | collective-permute-done | bytes 393248 | tf_op jit(solution)/shard_map/while/body/eval_jaxpr/ppermute | solution.py:14
  413.0 2.9 conditional.4
  419.9 15.4 %collective-permute-done = bf16[2,256,3,128]{3,1,2,0:T(8,128)(2,1)S(1)} collective-permute-done((bf16[2,256,3,128]{3,1,2,0:T(8,128)(2,1)}, bf16[2,256,3,128]{3,1,2,0:T(8,128)(2,1)S(1)}, u32[]{:S(2)}, u32[]{:S(2)}) %collective-permute-start) | collective-permute-done | bytes 393248 | tf_op jit(solution)/shard_map/while/body/eval_jaxpr/ppermute | solution.py:14
  439.2 15.4 %collective-permute-done = bf16[2,256,3,128]{3,1,2,0:T(8,128)(2,1)S(1)} collective-permute-done((bf16[2,256,3,128]{3,1,2,0:T(8,128)(2,1)}, bf16[2,256,3,128]{3,1,2,0:T(8,128)(2,1)S(1)}, u32[]{:S(2)}, u32[]{:S(2)}) %collective-permute-start) | collective-permute-done | bytes 393248 | tf_op jit(solution)/shard_map/while/body/eval_jaxpr/ppermute | solution.py:14
  458.5 15.4 %collective-permute-done = bf16[2,256,3,128]{3,1,2,0:T(8,128)(2,1)S(1)} collective-permute-done((bf16[2,256,3,128]{3,1,2,0:T(8,128)(2,1)}, bf16[2,256,3,128]{3,1,2,0:T(8,128)(2,1)S(1)}, u32[]{:S(2)}, u32[]{:S(2)}) %collective-permute-start) | collective-permute-done | bytes 393248 | tf_op jit(solution)/shard_map/while/body/eval_jaxpr/ppermute | solution.py:14
  477.8 15.4 %collective-permute-done = bf16[2,256,3,128]{3,1,2,0:T(8,128)(2,1)S(1)} collective-permute-done((bf16[2,256,3,128]{3,1,2,0:T(8,128)(2,1)}, bf16[2,256,3,128]{3,1,2,0:T(8,128)(2,1)S(1)}, u32[]{:S(2)}, u32[]{:S(2)}) %collective-permute-start) | collective-permute-done | bytes 393248 | tf_op jit(solution)/shard_map/while/body/eval_jaxpr/ppermute | solution.py:14
  497.2 15.4 %collective-permute-done = bf16[2,256,3,128]{3,1,2,0:T(8,128)(2,1)S(1)} collective-permute-done((bf16[2,256,3,128]{3,1,2,0:T(8,128)(2,1)}, bf16[2,256,3,128]{3,1,2,0:T(8,128)(2,1)S(1)}, u32[]{:S(2)}, u32[]{:S(2)}) %collective-permute-start) | collective-permute-done | bytes 393248 | tf_op jit(solution)/shard_map/while/body/eval_jaxpr/ppermute | solution.py:14
  516.5 15.4 %collective-permute-done = bf16[2,256,3,128]{3,1,2,0:T(8,128)(2,1)S(1)} collective-permute-done((bf16[2,256,3,128]{3,1,2,0:T(8,128)(2,1)}, bf16[2,256,3,128]{3,1,2,0:T(8,128)(2,1)S(1)}, u32[]{:S(2)}, u32[]{:S(2)}) %collective-permute-start) | collective-permute-done | bytes 393248 | tf_op jit(solution)/shard_map/while/body/eval_jaxpr/ppermute | solution.py:14
  535.8 15.5 %collective-permute-done = bf16[2,256,3,128]{3,1,2,0:T(8,128)(2,1)S(1)} collective-permute-done((bf16[2,256,3,128]{3,1,2,0:T(8,128)(2,1)}, bf16[2,256,3,128]{3,1,2,0:T(8,128)(2,1)S(1)}, u32[]{:S(2)}, u32[]{:S(2)}) %collective-permute-start) | collective-permute-done | bytes 393248 | tf_op jit(solution)/shard_map/while/body/eval_jaxpr/ppermute | solution.py:14
  555.2 16.5 %collective-permute-done = bf16[2,256,3,128]{3,1,2,0:T(8,128)(2,1)S(1)} collective-permute-done((bf16[2,256,3,128]{3,1,2,0:T(8,128)(2,1)}, bf16[2,256,3,128]{3,1,2,0:T(8,128)(2,1)S(1)}, u32[]{:S(2)}, u32[]{:S(2)}) %collective-permute-start) | collective-permute-done | bytes 393248 | tf_op jit(solution)/shard_map/while/body/eval_jaxpr/ppermute | solution.py:14
  575.7 19.1 %collective-permute-done = bf16[2,256,3,128]{3,1,2,0:T(8,128)(2,1)S(1)} collective-permute-done((bf16[2,256,3,128]{3,1,2,0:T(8,128)(2,1)}, bf16[2,256,3,128]{3,1,2,0:T(8,128)(2,1)S(1)}, u32[]{:S(2)}, u32[]{:S(2)}) %collective-permute-start) | collective-permute-done | bytes 393248 | tf_op jit(solution)/shard_map/while/body/eval_jaxpr/ppermute | solution.py:14
  598.7 18.9 %collective-permute-done = bf16[2,256,3,128]{3,1,2,0:T(8,128)(2,1)S(1)} collective-permute-done((bf16[2,256,3,128]{3,1,2,0:T(8,128)(2,1)}, bf16[2,256,3,128]{3,1,2,0:T(8,128)(2,1)S(1)}, u32[]{:S(2)}, u32[]{:S(2)}) %collective-permute-start) | collective-permute-done | bytes 393248 | tf_op jit(solution)/shard_map/while/body/eval_jaxpr/ppermute | solution.py:14
  621.6 18.7 %collective-permute-done = bf16[2,256,3,128]{3,1,2,0:T(8,128)(2,1)S(1)} collective-permute-done((bf16[2,256,3,128]{3,1,2,0:T(8,128)(2,1)}, bf16[2,256,3,128]{3,1,2,0:T(8,128)(2,1)S(1)}, u32[]{:S(2)}, u32[]{:S(2)}) %collective-permute-start) | collective-permute-done | bytes 393248 | tf_op jit(solution)/shard_map/while/body/eval_jaxpr/ppermute | solution.py:14
  644.2 18.5 %collective-permute-done = bf16[2,256,3,128]{3,1,2,0:T(8,128)(2,1)S(1)} collective-permute-done((bf16[2,256,3,128]{3,1,2,0:T(8,128)(2,1)}, bf16[2,256,3,128]{3,1,2,0:T(8,128)(2,1)S(1)}, u32[]{:S(2)}, u32[]{:S(2)}) %collective-permute-start) | collective-permute-done | bytes 393248 | tf_op jit(solution)/shard_map/while/body/eval_jaxpr/ppermute | solution.py:14
  662.8 2.9 conditional.4
  669.7 19.5 %collective-permute-done = bf16[2,256,3,128]{3,1,2,0:T(8,128)(2,1)S(1)} collective-permute-done((bf16[2,256,3,128]{3,1,2,0:T(8,128)(2,1)}, bf16[2,256,3,128]{3,1,2,0:T(8,128)(2,1)S(1)}, u32[]{:S(2)}, u32[]{:S(2)}) %collective-permute-start) | collective-permute-done | bytes 393248 | tf_op jit(solution)/shard_map/while/body/eval_jaxpr/ppermute | solution.py:14
  693.2 15.4 %collective-permute-done = bf16[2,256,3,128]{3,1,2,0:T(8,128)(2,1)S(1)} collective-permute-done((bf16[2,256,3,128]{3,1,2,0:T(8,128)(2,1)}, bf16[2,256,3,128]{3,1,2,0:T(8,128)(2,1)S(1)}, u32[]{:S(2)}, u32[]{:S(2)}) %collective-permute-start) | collective-permute-done | bytes 393248 | tf_op jit(solution)/shard_map/while/body/eval_jaxpr/ppermute | solution.py:14
  708.5 2.9 conditional.4
  715.4 15.4 %collective-permute-done = bf16[2,256,3,128]{3,1,2,0:T(8,128)(2,1)S(1)} collective-permute-done((bf16[2,256,3,128]{3,1,2,0:T(8,128)(2,1)}, bf16[2,256,3,128]{3,1,2,0:T(8,128)(2,1)S(1)}, u32[]{:S(2)}, u32[]{:S(2)}) %collective-permute-start) | collective-permute-done | bytes 393248 | tf_op jit(solution)/shard_map/while/body/eval_jaxpr/ppermute | solution.py:14
  730.8 2.9 conditional.4
  734.9 17.9 %all_to_all.69 = bf16[256,3,128]{2,1,0:T(4,128)(2,1)S(1)} all-to-all(bf16[256,3,128]{2,1,0:T(4,128)(2,1)S(1)} %fusion.25), channel_id=1, replica_groups=mesh['blk'=32,'head'=8,'batch'=2] {'head'}, dimensions={0} | all-to-all | bytes 393216 | tf_op jit(solution)/shard_map/all_to_all | solution.py:88
  (182 shorter events, 131.9 us)
Async XLA Ops:
  0.0 40.3 %copy-start = (bf16[32,3072]{1,0:T(8,128)(2,1)S(1)}, bf16[32,3072]{1,0:T(8,128)(2,1)}, u32[]{:S(2)}) copy-start(bf16[32,3072]{1,0:T(8,128)(2,1)} %param.14) | copy-start | bytes 589828
  2.9 33.0 %all-to-all-start.1 = ((bf16[32,24,128]{2,0,1:T(8,128)(2,1)}), bf16[32,24,128]{2,0,1:T(8,128)(2,1)S(1)}, u32[]{:S(2)}, u32[]{:S(2)}) async-start(bf16[32,24,128]{2,0,1:T(8,128)(2,1)} %copy_bitcast_fusion.2), calls=%async_computation.1 | async-start | bytes 393216 | tf_op jit(solution)/shard_map/all_to_all | solution.py:30
  35.8 20.5 %all-to-all-start = ((bf16[32,24,128]{2,0,1:T(8,128)(2,1)}), bf16[32,24,128]{2,0,1:T(8,128)(2,1)S(1)}, u32[]{:S(2)}, u32[]{:S(2)}) async-start(bf16[32,24,128]{2,0,1:T(8,128)(2,1)} %copy_bitcast_fusion.3), calls=%async_computation | async-start | bytes 393216 | tf_op jit(solution)/shard_map/all_to_all | solution.py:31
  56.3 20.1 %all-to-all-start.2 = ((bf16[32,24,128]{2,0,1:T(8,128)(2,1)}), bf16[32,24,128]{2,0,1:T(8,128)(2,1)S(1)}, u32[]{:S(2)}, u32[]{:S(2)}) async-start(bf16[32,24,128]{2,0,1:T(8,128)(2,1)} %copy_bitcast_fusion.1), calls=%async_computation.2 | async-start | bytes 393216 | tf_op jit(solution)/shard_map/all_to_all | solution.py:32
  80.7 18.6 %collective-permute-start = (bf16[2,256,3,128]{3,1,2,0:T(8,128)(2,1)}, bf16[2,256,3,128]{3,1,2,0:T(8,128)(2,1)S(1)}, u32[]{:S(2)}, u32[]{:S(2)}) collective-permute-start(bf16[2,256,3,128]{3,1,2,0:T(8,128)(2,1)} %get-tuple-element.398), channel_id=1, source_target_pairs={{496,0},{0,16},{16,32},{32,48},{48,64},{64,80},{80,96},{96,112},{1... | collective-permute-start | bytes 1179656 | tf_op jit(solution)/shard_map/while/body/eval_jaxpr/ppermute | solution.py:14
  100.1 18.6 %collective-permute-start = (bf16[2,256,3,128]{3,1,2,0:T(8,128)(2,1)}, bf16[2,256,3,128]{3,1,2,0:T(8,128)(2,1)S(1)}, u32[]{:S(2)}, u32[]{:S(2)}) collective-permute-start(bf16[2,256,3,128]{3,1,2,0:T(8,128)(2,1)} %get-tuple-element.398), channel_id=1, source_target_pairs={{496,0},{0,16},{16,32},{32,48},{48,64},{64,80},{80,96},{96,112},{1... | collective-permute-start | bytes 1179656 | tf_op jit(solution)/shard_map/while/body/eval_jaxpr/ppermute | solution.py:14
  119.4 18.6 %collective-permute-start = (bf16[2,256,3,128]{3,1,2,0:T(8,128)(2,1)}, bf16[2,256,3,128]{3,1,2,0:T(8,128)(2,1)S(1)}, u32[]{:S(2)}, u32[]{:S(2)}) collective-permute-start(bf16[2,256,3,128]{3,1,2,0:T(8,128)(2,1)} %get-tuple-element.398), channel_id=1, source_target_pairs={{496,0},{0,16},{16,32},{32,48},{48,64},{64,80},{80,96},{96,112},{1... | collective-permute-start | bytes 1179656 | tf_op jit(solution)/shard_map/while/body/eval_jaxpr/ppermute | solution.py:14
  141.6 18.6 %collective-permute-start = (bf16[2,256,3,128]{3,1,2,0:T(8,128)(2,1)}, bf16[2,256,3,128]{3,1,2,0:T(8,128)(2,1)S(1)}, u32[]{:S(2)}, u32[]{:S(2)}) collective-permute-start(bf16[2,256,3,128]{3,1,2,0:T(8,128)(2,1)} %get-tuple-element.398), channel_id=1, source_target_pairs={{496,0},{0,16},{16,32},{32,48},{48,64},{64,80},{80,96},{96,112},{1... | collective-permute-start | bytes 1179656 | tf_op jit(solution)/shard_map/while/body/eval_jaxpr/ppermute | solution.py:14
  160.9 18.6 %collective-permute-start = (bf16[2,256,3,128]{3,1,2,0:T(8,128)(2,1)}, bf16[2,256,3,128]{3,1,2,0:T(8,128)(2,1)S(1)}, u32[]{:S(2)}, u32[]{:S(2)}) collective-permute-start(bf16[2,256,3,128]{3,1,2,0:T(8,128)(2,1)} %get-tuple-element.398), channel_id=1, source_target_pairs={{496,0},{0,16},{16,32},{32,48},{48,64},{64,80},{80,96},{96,112},{1... | collective-permute-start | bytes 1179656 | tf_op jit(solution)/shard_map/while/body/eval_jaxpr/ppermute | solution.py:14
  183.2 19.0 %collective-permute-start = (bf16[2,256,3,128]{3,1,2,0:T(8,128)(2,1)}, bf16[2,256,3,128]{3,1,2,0:T(8,128)(2,1)S(1)}, u32[]{:S(2)}, u32[]{:S(2)}) collective-permute-start(bf16[2,256,3,128]{3,1,2,0:T(8,128)(2,1)} %get-tuple-element.398), channel_id=1, source_target_pairs={{496,0},{0,16},{16,32},{32,48},{48,64},{64,80},{80,96},{96,112},{1... | collective-permute-start | bytes 1179656 | tf_op jit(solution)/shard_map/while/body/eval_jaxpr/ppermute | solution.py:14
  202.9 20.1 %collective-permute-start = (bf16[2,256,3,128]{3,1,2,0:T(8,128)(2,1)}, bf16[2,256,3,128]{3,1,2,0:T(8,128)(2,1)S(1)}, u32[]{:S(2)}, u32[]{:S(2)}) collective-permute-start(bf16[2,256,3,128]{3,1,2,0:T(8,128)(2,1)} %get-tuple-element.398), channel_id=1, source_target_pairs={{496,0},{0,16},{16,32},{32,48},{48,64},{64,80},{80,96},{96,112},{1... | collective-permute-start | bytes 1179656 | tf_op jit(solution)/shard_map/while/body/eval_jaxpr/ppermute | solution.py:14
  223.7 21.3 %collective-permute-start = (bf16[2,256,3,128]{3,1,2,0:T(8,128)(2,1)}, bf16[2,256,3,128]{3,1,2,0:T(8,128)(2,1)S(1)}, u32[]{:S(2)}, u32[]{:S(2)}) collective-permute-start(bf16[2,256,3,128]{3,1,2,0:T(8,128)(2,1)} %get-tuple-element.398), channel_id=1, source_target_pairs={{496,0},{0,16},{16,32},{32,48},{48,64},{64,80},{80,96},{96,112},{1... | collective-permute-start | bytes 1179656 | tf_op jit(solution)/shard_map/while/body/eval_jaxpr/ppermute | solution.py:14
  245.7 22.4 %collective-permute-start = (bf16[2,256,3,128]{3,1,2,0:T(8,128)(2,1)}, bf16[2,256,3,128]{3,1,2,0:T(8,128)(2,1)S(1)}, u32[]{:S(2)}, u32[]{:S(2)}) collective-permute-start(bf16[2,256,3,128]{3,1,2,0:T(8,128)(2,1)} %get-tuple-element.398), channel_id=1, source_target_pairs={{496,0},{0,16},{16,32},{32,48},{48,64},{64,80},{80,96},{96,112},{1... | collective-permute-start | bytes 1179656 | tf_op jit(solution)/shard_map/while/body/eval_jaxpr/ppermute | solution.py:14
  268.9 22.0 %collective-permute-start = (bf16[2,256,3,128]{3,1,2,0:T(8,128)(2,1)}, bf16[2,256,3,128]{3,1,2,0:T(8,128)(2,1)S(1)}, u32[]{:S(2)}, u32[]{:S(2)}) collective-permute-start(bf16[2,256,3,128]{3,1,2,0:T(8,128)(2,1)} %get-tuple-element.398), channel_id=1, source_target_pairs={{496,0},{0,16},{16,32},{32,48},{48,64},{64,80},{80,96},{96,112},{1... | collective-permute-start | bytes 1179656 | tf_op jit(solution)/shard_map/while/body/eval_jaxpr/ppermute | solution.py:14
  291.7 21.2 %collective-permute-start = (bf16[2,256,3,128]{3,1,2,0:T(8,128)(2,1)}, bf16[2,256,3,128]{3,1,2,0:T(8,128)(2,1)S(1)}, u32[]{:S(2)}, u32[]{:S(2)}) collective-permute-start(bf16[2,256,3,128]{3,1,2,0:T(8,128)(2,1)} %get-tuple-element.398), channel_id=1, source_target_pairs={{496,0},{0,16},{16,32},{32,48},{48,64},{64,80},{80,96},{96,112},{1... | collective-permute-start | bytes 1179656 | tf_op jit(solution)/shard_map/while/body/eval_jaxpr/ppermute | solution.py:14
  313.6 20.3 %collective-permute-start = (bf16[2,256,3,128]{3,1,2,0:T(8,128)(2,1)}, bf16[2,256,3,128]{3,1,2,0:T(8,128)(2,1)S(1)}, u32[]{:S(2)}, u32[]{:S(2)}) collective-permute-start(bf16[2,256,3,128]{3,1,2,0:T(8,128)(2,1)} %get-tuple-element.398), channel_id=1, source_target_pairs={{496,0},{0,16},{16,32},{32,48},{48,64},{64,80},{80,96},{96,112},{1... | collective-permute-start | bytes 1179656 | tf_op jit(solution)/shard_map/while/body/eval_jaxpr/ppermute | solution.py:14
  334.6 19.5 %collective-permute-start = (bf16[2,256,3,128]{3,1,2,0:T(8,128)(2,1)}, bf16[2,256,3,128]{3,1,2,0:T(8,128)(2,1)S(1)}, u32[]{:S(2)}, u32[]{:S(2)}) collective-permute-start(bf16[2,256,3,128]{3,1,2,0:T(8,128)(2,1)} %get-tuple-element.398), channel_id=1, source_target_pairs={{496,0},{0,16},{16,32},{32,48},{48,64},{64,80},{80,96},{96,112},{1... | collective-permute-start | bytes 1179656 | tf_op jit(solution)/shard_map/while/body/eval_jaxpr/ppermute | solution.py:14
  354.8 18.6 %collective-permute-start = (bf16[2,256,3,128]{3,1,2,0:T(8,128)(2,1)}, bf16[2,256,3,128]{3,1,2,0:T(8,128)(2,1)S(1)}, u32[]{:S(2)}, u32[]{:S(2)}) collective-permute-start(bf16[2,256,3,128]{3,1,2,0:T(8,128)(2,1)} %get-tuple-element.398), channel_id=1, source_target_pairs={{496,0},{0,16},{16,32},{32,48},{48,64},{64,80},{80,96},{96,112},{1... | collective-permute-start | bytes 1179656 | tf_op jit(solution)/shard_map/while/body/eval_jaxpr/ppermute | solution.py:14
  374.2 18.6 %collective-permute-start = (bf16[2,256,3,128]{3,1,2,0:T(8,128)(2,1)}, bf16[2,256,3,128]{3,1,2,0:T(8,128)(2,1)S(1)}, u32[]{:S(2)}, u32[]{:S(2)}) collective-permute-start(bf16[2,256,3,128]{3,1,2,0:T(8,128)(2,1)} %get-tuple-element.398), channel_id=1, source_target_pairs={{496,0},{0,16},{16,32},{32,48},{48,64},{64,80},{80,96},{96,112},{1... | collective-permute-start | bytes 1179656 | tf_op jit(solution)/shard_map/while/body/eval_jaxpr/ppermute | solution.py:14
  393.5 19.5 %collective-permute-start = (bf16[2,256,3,128]{3,1,2,0:T(8,128)(2,1)}, bf16[2,256,3,128]{3,1,2,0:T(8,128)(2,1)S(1)}, u32[]{:S(2)}, u32[]{:S(2)}) collective-permute-start(bf16[2,256,3,128]{3,1,2,0:T(8,128)(2,1)} %get-tuple-element.398), channel_id=1, source_target_pairs={{496,0},{0,16},{16,32},{32,48},{48,64},{64,80},{80,96},{96,112},{1... | collective-permute-start | bytes 1179656 | tf_op jit(solution)/shard_map/while/body/eval_jaxpr/ppermute | solution.py:14
  416.6 18.6 %collective-permute-start = (bf16[2,256,3,128]{3,1,2,0:T(8,128)(2,1)}, bf16[2,256,3,128]{3,1,2,0:T(8,128)(2,1)S(1)}, u32[]{:S(2)}, u32[]{:S(2)}) collective-permute-start(bf16[2,256,3,128]{3,1,2,0:T(8,128)(2,1)} %get-tuple-element.398), channel_id=1, source_target_pairs={{496,0},{0,16},{16,32},{32,48},{48,64},{64,80},{80,96},{96,112},{1... | collective-permute-start | bytes 1179656 | tf_op jit(solution)/shard_map/while/body/eval_jaxpr/ppermute | solution.py:14
  436.0 18.6 %collective-permute-start = (bf16[2,256,3,128]{3,1,2,0:T(8,128)(2,1)}, bf16[2,256,3,128]{3,1,2,0:T(8,128)(2,1)S(1)}, u32[]{:S(2)}, u32[]{:S(2)}) collective-permute-start(bf16[2,256,3,128]{3,1,2,0:T(8,128)(2,1)} %get-tuple-element.398), channel_id=1, source_target_pairs={{496,0},{0,16},{16,32},{32,48},{48,64},{64,80},{80,96},{96,112},{1... | collective-permute-start | bytes 1179656 | tf_op jit(solution)/shard_map/while/body/eval_jaxpr/ppermute | solution.py:14
  455.3 18.6 %collective-permute-start = (bf16[2,256,3,128]{3,1,2,0:T(8,128)(2,1)}, bf16[2,256,3,128]{3,1,2,0:T(8,128)(2,1)S(1)}, u32[]{:S(2)}, u32[]{:S(2)}) collective-permute-start(bf16[2,256,3,128]{3,1,2,0:T(8,128)(2,1)} %get-tuple-element.398), channel_id=1, source_target_pairs={{496,0},{0,16},{16,32},{32,48},{48,64},{64,80},{80,96},{96,112},{1... | collective-permute-start | bytes 1179656 | tf_op jit(solution)/shard_map/while/body/eval_jaxpr/ppermute | solution.py:14
  474.6 18.6 %collective-permute-start = (bf16[2,256,3,128]{3,1,2,0:T(8,128)(2,1)}, bf16[2,256,3,128]{3,1,2,0:T(8,128)(2,1)S(1)}, u32[]{:S(2)}, u32[]{:S(2)}) collective-permute-start(bf16[2,256,3,128]{3,1,2,0:T(8,128)(2,1)} %get-tuple-element.398), channel_id=1, source_target_pairs={{496,0},{0,16},{16,32},{32,48},{48,64},{64,80},{80,96},{96,112},{1... | collective-permute-start | bytes 1179656 | tf_op jit(solution)/shard_map/while/body/eval_jaxpr/ppermute | solution.py:14
  493.9 18.6 %collective-permute-start = (bf16[2,256,3,128]{3,1,2,0:T(8,128)(2,1)}, bf16[2,256,3,128]{3,1,2,0:T(8,128)(2,1)S(1)}, u32[]{:S(2)}, u32[]{:S(2)}) collective-permute-start(bf16[2,256,3,128]{3,1,2,0:T(8,128)(2,1)} %get-tuple-element.398), channel_id=1, source_target_pairs={{496,0},{0,16},{16,32},{32,48},{48,64},{64,80},{80,96},{96,112},{1... | collective-permute-start | bytes 1179656 | tf_op jit(solution)/shard_map/while/body/eval_jaxpr/ppermute | solution.py:14
  513.3 18.6 %collective-permute-start = (bf16[2,256,3,128]{3,1,2,0:T(8,128)(2,1)}, bf16[2,256,3,128]{3,1,2,0:T(8,128)(2,1)S(1)}, u32[]{:S(2)}, u32[]{:S(2)}) collective-permute-start(bf16[2,256,3,128]{3,1,2,0:T(8,128)(2,1)} %get-tuple-element.398), channel_id=1, source_target_pairs={{496,0},{0,16},{16,32},{32,48},{48,64},{64,80},{80,96},{96,112},{1... | collective-permute-start | bytes 1179656 | tf_op jit(solution)/shard_map/while/body/eval_jaxpr/ppermute | solution.py:14
  532.6 18.7 %collective-permute-start = (bf16[2,256,3,128]{3,1,2,0:T(8,128)(2,1)}, bf16[2,256,3,128]{3,1,2,0:T(8,128)(2,1)S(1)}, u32[]{:S(2)}, u32[]{:S(2)}) collective-permute-start(bf16[2,256,3,128]{3,1,2,0:T(8,128)(2,1)} %get-tuple-element.398), channel_id=1, source_target_pairs={{496,0},{0,16},{16,32},{32,48},{48,64},{64,80},{80,96},{96,112},{1... | collective-permute-start | bytes 1179656 | tf_op jit(solution)/shard_map/while/body/eval_jaxpr/ppermute | solution.py:14
  552.0 19.7 %collective-permute-start = (bf16[2,256,3,128]{3,1,2,0:T(8,128)(2,1)}, bf16[2,256,3,128]{3,1,2,0:T(8,128)(2,1)S(1)}, u32[]{:S(2)}, u32[]{:S(2)}) collective-permute-start(bf16[2,256,3,128]{3,1,2,0:T(8,128)(2,1)} %get-tuple-element.398), channel_id=1, source_target_pairs={{496,0},{0,16},{16,32},{32,48},{48,64},{64,80},{80,96},{96,112},{1... | collective-permute-start | bytes 1179656 | tf_op jit(solution)/shard_map/while/body/eval_jaxpr/ppermute | solution.py:14
  572.5 22.3 %collective-permute-start = (bf16[2,256,3,128]{3,1,2,0:T(8,128)(2,1)}, bf16[2,256,3,128]{3,1,2,0:T(8,128)(2,1)S(1)}, u32[]{:S(2)}, u32[]{:S(2)}) collective-permute-start(bf16[2,256,3,128]{3,1,2,0:T(8,128)(2,1)} %get-tuple-element.398), channel_id=1, source_target_pairs={{496,0},{0,16},{16,32},{32,48},{48,64},{64,80},{80,96},{96,112},{1... | collective-permute-start | bytes 1179656 | tf_op jit(solution)/shard_map/while/body/eval_jaxpr/ppermute | solution.py:14
  595.5 22.1 %collective-permute-start = (bf16[2,256,3,128]{3,1,2,0:T(8,128)(2,1)}, bf16[2,256,3,128]{3,1,2,0:T(8,128)(2,1)S(1)}, u32[]{:S(2)}, u32[]{:S(2)}) collective-permute-start(bf16[2,256,3,128]{3,1,2,0:T(8,128)(2,1)} %get-tuple-element.398), channel_id=1, source_target_pairs={{496,0},{0,16},{16,32},{32,48},{48,64},{64,80},{80,96},{96,112},{1... | collective-permute-start | bytes 1179656 | tf_op jit(solution)/shard_map/while/body/eval_jaxpr/ppermute | solution.py:14
  618.3 21.9 %collective-permute-start = (bf16[2,256,3,128]{3,1,2,0:T(8,128)(2,1)}, bf16[2,256,3,128]{3,1,2,0:T(8,128)(2,1)S(1)}, u32[]{:S(2)}, u32[]{:S(2)}) collective-permute-start(bf16[2,256,3,128]{3,1,2,0:T(8,128)(2,1)} %get-tuple-element.398), channel_id=1, source_target_pairs={{496,0},{0,16},{16,32},{32,48},{48,64},{64,80},{80,96},{96,112},{1... | collective-permute-start | bytes 1179656 | tf_op jit(solution)/shard_map/while/body/eval_jaxpr/ppermute | solution.py:14
  641.0 21.8 %collective-permute-start = (bf16[2,256,3,128]{3,1,2,0:T(8,128)(2,1)}, bf16[2,256,3,128]{3,1,2,0:T(8,128)(2,1)S(1)}, u32[]{:S(2)}, u32[]{:S(2)}) collective-permute-start(bf16[2,256,3,128]{3,1,2,0:T(8,128)(2,1)} %get-tuple-element.398), channel_id=1, source_target_pairs={{496,0},{0,16},{16,32},{32,48},{48,64},{64,80},{80,96},{96,112},{1... | collective-permute-start | bytes 1179656 | tf_op jit(solution)/shard_map/while/body/eval_jaxpr/ppermute | solution.py:14
  666.4 22.8 %collective-permute-start = (bf16[2,256,3,128]{3,1,2,0:T(8,128)(2,1)}, bf16[2,256,3,128]{3,1,2,0:T(8,128)(2,1)S(1)}, u32[]{:S(2)}, u32[]{:S(2)}) collective-permute-start(bf16[2,256,3,128]{3,1,2,0:T(8,128)(2,1)} %get-tuple-element.398), channel_id=1, source_target_pairs={{496,0},{0,16},{16,32},{32,48},{48,64},{64,80},{80,96},{96,112},{1... | collective-permute-start | bytes 1179656 | tf_op jit(solution)/shard_map/while/body/eval_jaxpr/ppermute | solution.py:14
  689.9 18.6 %collective-permute-start = (bf16[2,256,3,128]{3,1,2,0:T(8,128)(2,1)}, bf16[2,256,3,128]{3,1,2,0:T(8,128)(2,1)S(1)}, u32[]{:S(2)}, u32[]{:S(2)}) collective-permute-start(bf16[2,256,3,128]{3,1,2,0:T(8,128)(2,1)} %get-tuple-element.398), channel_id=1, source_target_pairs={{496,0},{0,16},{16,32},{32,48},{48,64},{64,80},{80,96},{96,112},{1... | collective-permute-start | bytes 1179656 | tf_op jit(solution)/shard_map/while/body/eval_jaxpr/ppermute | solution.py:14
  712.2 18.6 %collective-permute-start = (bf16[2,256,3,128]{3,1,2,0:T(8,128)(2,1)}, bf16[2,256,3,128]{3,1,2,0:T(8,128)(2,1)S(1)}, u32[]{:S(2)}, u32[]{:S(2)}) collective-permute-start(bf16[2,256,3,128]{3,1,2,0:T(8,128)(2,1)} %get-tuple-element.398), channel_id=1, source_target_pairs={{496,0},{0,16},{16,32},{32,48},{48,64},{64,80},{80,96},{96,112},{1... | collective-permute-start | bytes 1179656 | tf_op jit(solution)/shard_map/while/body/eval_jaxpr/ppermute | solution.py:14
where the time goes:
time: 757 us; the launch traced here: 754 us
  waiting for transfers between devices  552 us (73%)
  starting transfers between devices  87.8 us (12%)
  other arithmetic  41.7 us (6%)
  local copies, waits for them, and re-layouts  29.1 us (4%)
  loops' own time  19 us (3%)
  blocking collectives  17.9 us (2%)
    ppermute x31, waiting for transfers between devices, shifted(): return lax.ppermute(block, axis, route)  512 us
    ppermute x31, starting transfers between devices, shifted(): return lax.ppermute(block, axis, route)  60.7 us
    while x31, local copies, waits for them, and re-layouts  22.9 us
    reduce_or x32, other arithmetic, absorb(): return lax.cond(jnp.any(allowed), attend, keep_state, state_now)  22.7 us
    another operation x1, loops' own time, per_device(): lax.fori_loop(1, cycle_size, cycle_turn, (own_state, kv_pair))  18.9 us
    all_to_all x1, starting transfers between devices, per_device(): lax.all_to_all(q_local, 'head', split_axis=1, concat_axis=0, tiled=True)  18 us
    all_to_all x1, blocking collectives, per_device(): lax.all_to_all(mixed, 'head', split_axis=0, concat_axis=1, tiled=True)  17.9 us
    all_to_all x1, waiting for transfers between devices, per_device(): lax.all_to_all(k_local, 'head', split_axis=1, concat_axis=0, tiled=True)  15.3 us
  transfers between devices with their start and end apart: 34, of which 34 were waited for; matrix products, arithmetic and copies ran while one was open for 4% of the time, Pallas kernels for 0%

commit v1 on v0

v1 whole, which is shorter than its diff:
```python
import functools
import math

import jax
import jax.numpy as jnp
from jax import lax
from jax.experimental import pallas as pl
from jax.experimental.pallas import tpu as pltpu
from jax.sharding import PartitionSpec as P

HEADS = 24
HDIM = 128
GROUP = 3
COLS = GROUP * HDIM
NEG = -1e30
MESH = pl.DeviceIdType.MESH


def normalize(inputs, weights):
    widened = inputs.astype(jnp.float32)
    mean_square = jnp.mean(widened * widened, axis=-1, keepdims=True)
    return (widened * lax.rsqrt(mean_square + 1e-06) * weights).astype(jnp.bfloat16)


def kernel(
    q_in, k_in, v_in, qg, kg, mask, out,
    sent, kv, q_all, bias, run_max, run_sum, acc, mixed,
    a_send, a_recv, h_send, h_recv, r_send, r_recv, p_send, p_recv, o_send, o_recv,
):
    blk, head, c = lax.axis_index("blk"), lax.axis_index("head"), lax.axis_index("batch")
    zl, y = blk // 4, blk % 4
    x, zh = head // 2, head % 2
    place = zh * 8 + zl
    clip = x % 2
    group = (x // 2) * 4 + y

    def device(xx, yy, zz, cc):
        return {"blk": (zz % 8) * 4 + yy, "head": xx * 2 + zz // 8, "batch": cc}

    my_core = y // 2
    takers = [(2 * (t // 4) + c, t % 4, my_core) for t in range(8)]
    holders = [(s % 4, 2 * c + s // 4, clip) for s in range(8)]

    def is_me(d):
        return (d[0] == x) & (d[1] == y) & (d[2] == c)

    step_to = jnp.where(c == 0, 1, 15)
    ahead = device(x, y, (place + step_to) % 16, c)
    behind = device(x, y, (place + 16 - step_to) % 16, c)
    partner = device(x, y, place, 1 - c)

    barrier = pltpu.get_barrier_semaphore()
    for d in takers + holders:
        @pl.when(jnp.logical_not(is_me(d)))
        def _(d=d):
            pl.semaphore_signal(barrier, inc=1, device_id=device(d[0], d[1], place, d[2]), device_id_type=MESH)
    for d in (ahead, behind, partner):
        pl.semaphore_signal(barrier, inc=1, device_id=d, device_id_type=MESH)

    sent[0] = v_in[...]
    sent[1] = normalize(k_in[...], kg[...])
    sent[2] = normalize(q_in[...], qg[...])

    tiles = mask.shape[0]
    q_tile = zl * 8 + c * 4 + lax.broadcasted_iota(jnp.int32, (tiles, 256), 1) // 64
    pick = (lax.broadcasted_iota(jnp.int32, (tiles, 256), 0) == q_tile).astype(jnp.float32)
    live = lax.dot_general(
        mask[...].astype(jnp.float32), pick, (((0,), (0,)), ((), ())), preferred_element_type=jnp.float32
    )
    bias[...] = jnp.where(live > 0.5, 0.0, NEG)

    self_pair = ((x % 2) == c) & (my_core == c)
    pl.semaphore_wait(barrier, 19 - 2 * self_pair.astype(jnp.int32))

    my_index = (y % 2) * 4 + x
    my_row = pl.multiple_of(y * 128 + x * 32, 32)
    my_q_row = pl.multiple_of((y % 2) * 128 + x * 32, 32)

    def a_dst(kind):
        if kind == 2:
            return q_all.at[pl.ds(my_q_row, 32), :]
        return kv.at[0, 1 - kind, pl.ds(my_row, 32), :]

    def a_copy(kind, t):
        d = takers[t]
        cols = (d[0] // 2 * 4 + d[1]) * COLS
        return pltpu.make_async_remote_copy(
            src_ref=sent.at[kind, :, pl.ds(pl.multiple_of(cols, 128), COLS)],
            dst_ref=a_dst(kind),
            send_sem=a_send.at[kind, t],
            recv_sem=a_recv.at[kind, my_index],
            device_id=device(d[0], d[1], place, d[2]),
            device_id_type=MESH,
        )

    def a_local(kind, t):
        d = takers[t]
        cols = (d[0] // 2 * 4 + d[1]) * COLS
        return pltpu.make_async_copy(
            sent.at[kind, :, pl.ds(pl.multiple_of(cols, 128), COLS)], a_dst(kind), a_recv.at[kind, my_index]
        )

    for kind in range(3):
        for t in range(8):
            mine = is_me(takers[t])

            @pl.when(jnp.logical_not(mine))
            def _(kind=kind, t=t):
                a_copy(kind, t).start()

            @pl.when(mine)
            def _(kind=kind, t=t):
                a_local(kind, t).start()

    def await_rows(kind):
        for s in range(8):
            if kind == 2:
                dst = q_all.at[pl.ds(s * 32, 32), :]
            else:
                dst = kv.at[0, 1 - kind, pl.ds(pl.multiple_of(c * 256 + s * 32, 32), 32), :]
            pltpu.make_async_copy(dst, dst, a_recv.at[kind, s]).wait()

    def half(i, core):
        rows = pl.ds(pl.multiple_of(core * 256, 256), 256)
        return pltpu.make_async_remote_copy(
            src_ref=kv.at[0, i, rows, :], dst_ref=kv.at[0, i, rows, :], send_sem=h_send.at[i], recv_sem=h_recv.at[i],
            device_id=partner, device_id_type=MESH,
        )

    def onward(s, i):
        return pltpu.make_async_remote_copy(
            src_ref=kv.at[s, i], dst_ref=kv.at[s + 1, i], send_sem=r_send.at[s, i], recv_sem=r_recv.at[s + 1, i],
            device_id=ahead, device_id_type=MESH,
        )

    def across(s, i, slot):
        return pltpu.make_async_remote_copy(
            src_ref=kv.at[s, i], dst_ref=kv.at[slot, i], send_sem=p_send.at[s, i], recv_sem=p_recv.at[s, i],
            device_id=partner, device_id_type=MESH,
        )

    def arrived(s, i):
        pltpu.make_async_copy(kv.at[s, i], kv.at[s, i], r_recv.at[s, i]).wait()

    def crossed(s, i, slot):
        pltpu.make_async_copy(kv.at[slot, i], kv.at[slot, i], p_recv.at[s, i]).wait()

    await_rows(0)
    half(1, c).start()
    await_rows(1)
    half(0, c).start()
    half(1, 1 - c).wait_recv()
    onward(0, 1).start()
    half(0, 1 - c).wait_recv()
    onward(0, 0).start()
    await_rows(2)

    scale = HDIM ** (-0.5) * math.log2(math.e)
    run_max[...] = jnp.full(run_max.shape, 2.0 * NEG, jnp.float32)
    run_sum[...] = jnp.zeros(run_sum.shape, jnp.float32)
    acc[...] = jnp.zeros(acc.shape, jnp.float32)

    def attend(slot, source):
        tile_bias = bias[pl.ds(pl.multiple_of((source % 8) * 8, 8), 8), :]
        for h in range(GROUP):
            cols = slice(h * HDIM, (h + 1) * HDIM)
            scores = lax.dot_general(
                kv[slot, 0, :, cols], q_all[:, cols], (((1,), (1,)), ((), ())), preferred_element_type=jnp.float32
            )
            scores = scores.reshape(8, 64, 256) * scale + tile_bias[:, None, :]
            scores = scores.reshape(512, 256)
            old_max = run_max[h]
            new_max = jnp.maximum(old_max, jnp.max(scores, axis=0, keepdims=True))
            weights = jnp.exp2(scores - new_max)
            rescale = jnp.exp2(old_max - new_max)
            run_max[h] = new_max
            run_sum[h] = run_sum[h] * rescale + jnp.sum(weights, axis=0, keepdims=True)
            product = lax.dot_general(
                kv[slot, 1, :, cols], weights.astype(jnp.bfloat16), (((0,), (0,)), ((), ())),
                preferred_element_type=jnp.float32,
            )
            acc[h] = acc[h] * rescale + product

    attend(0, place)

    def turn(s, carry):
        for i in (1, 0):
            arrived(s, i)

            @pl.when((s < 7) | (i == c))
            def _():
                onward(s, i).start()

            across(s, i, s + 8).start()
        attend(s, place + 16 - step_to * s % 16)
        for i in (1, 0):
            crossed(s, i, s + 8)
        attend(s + 8, place + step_to * s)
        return carry

    lax.fori_loop(1, 8, turn, 0)

    arrived(8, c)
    across(8, c, 8).start()
    crossed(8, 1 - c, 8)
    attend(8, place + 8)

    for h in range(GROUP):
        mixed[:, h * HDIM:(h + 1) * HDIM] = jnp.transpose(acc[h] / run_sum[h]).astype(jnp.bfloat16)

    def o_dst():
        return out.at[:, pl.ds(pl.multiple_of(group * COLS, 128), COLS)]

    def o_copy(s):
        d = holders[s]
        return pltpu.make_async_remote_copy(
            src_ref=mixed.at[pl.ds(s * 32, 32), :], dst_ref=o_dst(), send_sem=o_send.at[s], recv_sem=o_recv.at[group],
            device_id=device(d[0], d[1], place, d[2]), device_id_type=MESH,
        )

    def o_local(s):
        return pltpu.make_async_copy(mixed.at[pl.ds(s * 32, 32), :], o_dst(), o_recv.at[group])

    for s in range(8):
        mine = is_me(holders[s])

        @pl.when(jnp.logical_not(mine))
        def _(s=s):
            o_copy(s).start()

        @pl.when(mine)
        def _(s=s):
            o_local(s).start()

    for kind in range(3):
        for t in range(8):
            @pl.when(jnp.logical_not(is_me(takers[t])))
            def _(kind=kind, t=t):
                a_copy(kind, t).wait_send()
    for i in range(2):
        half(i, c).wait_send()
        onward(0, i).wait_send()

    def drain(s, carry):
        for i in range(2):
            @pl.when((s < 7) | (i == c))
            def _():
                onward(s, i).wait_send()

            across(s, i, s + 8).wait_send()
        return carry

    lax.fori_loop(1, 8, drain, 0)
    across(8, c, 8).wait_send()
    for s in range(8):
        @pl.when(jnp.logical_not(is_me(holders[s])))
        def _(s=s):
            o_copy(s).wait_send()
    for g in range(8):
        dst = out.at[:, g * COLS:(g + 1) * COLS]
        pltpu.make_async_copy(dst, dst, o_recv.at[g]).wait()


def per_device(query_rows, key_rows, value_rows, q_gain, k_gain, tile_mask):
    rows, width = query_rows.shape
    bf16, f32 = jnp.bfloat16, jnp.float32
    vmem = pl.BlockSpec(memory_space=pltpu.VMEM)
    dma = pltpu.SemaphoreType.DMA
    return pl.pallas_call(
        kernel,
        out_shape=jax.ShapeDtypeStruct((rows, width), bf16),
        in_specs=[vmem] * 6,
        out_specs=vmem,
        scratch_shapes=[
            pltpu.VMEM((3, rows, width), bf16),
            pltpu.VMEM((16, 2, 512, COLS), bf16),
            pltpu.VMEM((256, COLS), bf16),
            pltpu.VMEM((64, 256), f32),
            pltpu.VMEM((GROUP, 1, 256), f32),
            pltpu.VMEM((GROUP, 1, 256), f32),
            pltpu.VMEM((GROUP, HDIM, 256), f32),
            pltpu.VMEM((256, COLS), bf16),
            dma((3, 8)), dma((3, 8)),
            dma((2,)), dma((2,)),
            dma((9, 2)), dma((9, 2)),
            dma((9, 2)), dma((9, 2)),
            dma((8,)), dma((8,)),
        ],
        compiler_params=pltpu.CompilerParams(
            collective_id=0, has_side_effects=True, vmem_limit_bytes=48 * 1024 * 1024
        ),
    )(query_rows, key_rows, value_rows, q_gain.reshape(1, width), k_gain.reshape(1, width), tile_mask)


def solution(mesh):
    rows = P(("batch", "blk", "head"), None)
    return jax.shard_map(
        per_device,
        mesh=mesh,
        in_specs=(rows, rows, rows, P(), P(), P()),
        out_specs=rows,
        check_vma=False,
    )
```

time: 757 us -> 106 us (0.14)
  waiting for transfers between devices: 552 us -> 0 us
  Pallas kernels: 0 us -> 98.1 us
  starting transfers between devices: 87.8 us -> 0 us
  other arithmetic: 41.7 us -> 0 us
  local copies, waits for them, and re-layouts: 29.1 us -> 5.63 us
  loops' own time: 19 us -> 0 us
  blocking collectives: 17.9 us -> 0 us
    ppermute x31 -> x0, waiting for transfers between devices: 512 us -> none  [shifted(): return lax.ppermute(block, axis, route)]
    pallas_call x0 -> x1, Pallas kernels: none -> 98.1 us  [per_device(): pl.pallas_call(kernel, out_shape=jax.ShapeDtypeStruct((rows, width), bf16...]
    ppermute x31 -> x0, starting transfers between devices: 60.7 us -> none  [shifted(): return lax.ppermute(block, axis, route)]
    all_to_all x3 -> x0, waiting for transfers between devices: 40 us -> none  [the longest x1 15.3 us: per_device(): lax.all_to_all(k_local, 'head', split_axis=1, concat_axis=0, tiled=True)]
    all_to_all x3 -> x0, starting transfers between devices: 27.1 us -> none  [the longest x1 18 us: per_device(): lax.all_to_all(q_local, 'head', split_axis=1, concat_axis=0, tiled=True)]
    while x31 -> x0, local copies, waits for them, and re-layouts: 22.9 us -> none
    reduce_or x32 -> x0, other arithmetic: 22.7 us -> none  [absorb(): return lax.cond(jnp.any(allowed), attend, keep_state, state_now)]
    another operation x33 -> x0, loops' own time: 19 us -> none  [the longest x1 18.9 us: per_device(): lax.fori_loop(1, cycle_size, cycle_turn, (own_state, kv_pair))]
  transfers between devices with their start and end apart: 34 -> 0, of which waited for: 34 -> 0; matrix products, arithmetic and copies ran while one was open for 4% -> 0% of each run, Pallas kernels for 0% -> 0%
where the time goes in v1:
time: 106 us; the launch traced here: 104 us
  Pallas kernels  98.1 us (93%)
  local copies, waits for them, and re-layouts  5.63 us (5%)
    pallas_call x1, Pallas kernels, per_device(): pl.pallas_call(kernel, out_shape=jax.ShapeDtypeStruct((rows, width), bf16...  98.1 us
    unnamed x13, local copies, waits for them, and re-layouts  5.63 us

profile of v1, /device:TPU:6, one launch (start us, length us, event | category | flops | bytes accessed | tf_op | source)
XLA Modules:
  0.0 103.7 jit_solution(16599987106946109769)
XLA Ops:
  0.0 0.0 copy-start
  0.0 0.9 copy-done
  0.9 0.0 copy-start.1
  0.9 0.9 copy-done.1
  1.9 0.0 copy-start.2
  1.9 0.9 copy-done.2
  2.8 0.0 copy-start.3
  2.8 0.8 copy-done.3
  3.5 0.0 copy-start.4
  3.5 0.7 copy-done.4
  4.2 0.0 copy-start.5
  4.3 0.7 copy-done.5
  5.0 98.1 %shard_map.64 = bf16[32,3072]{1,0:T(8,128)(2,1)S(1)} custom-call(bf16[32,3072]{1,0:T(8,128)(2,1)S(1)} %copy-done, bf16[32,3072]{1,0:T(8,128)(2,1)S(1)} %copy-done.1, bf16[32,3072]{1,0:T(8,128)(2,1)S(1)} %copy-done.2, f32[1,3072]{1,0:T(1,128)S(1)} %bitcast.2, f32[1,3072]{1,0:T(1,128)S(1)} %bitcast.3, s32[64,64]{1,0:T(8,128)S(1)} %copy-done.3), custom_call_target="tpu_custom_call" | custom-call | tf_op jit(solution)/shard_map/pallas_call | solution.py:269
  103.1 0.7 copy.8
Async XLA Ops:
  0.0 0.9 copy-start
  0.9 0.9 copy-start.1
  1.9 0.9 copy-start.2
  2.8 0.8 copy-start.3
  3.5 0.7 copy-start.4
  4.2 0.7 copy-start.5

commit v2 on v1

v2 whole, which is shorter than its diff:
```python
import functools
import math

import jax
import jax.numpy as jnp
from jax import lax
from jax.experimental import pallas as pl
from jax.experimental.pallas import tpu as pltpu
from jax.sharding import PartitionSpec as P

HEADS = 24
HDIM = 128
GROUP = 3
COLS = GROUP * HDIM
NEG = -1e30
MESH = pl.DeviceIdType.MESH


def normalize(inputs, weights):
    widened = inputs.astype(jnp.float32)
    mean_square = jnp.mean(widened * widened, axis=-1, keepdims=True)
    return (widened * lax.rsqrt(mean_square + 1e-06) * weights).astype(jnp.bfloat16)


def kernel(
    q_in, k_in, v_in, qg, kg, mask, out,
    rows_in, sent, mine, theirs, q_all, bias, run_max, run_sum, acc, mixed,
    l_sem, a_send, a_recv, r_send, r_recv, p_send, p_recv, o_send, o_recv,
):
    blk, head, c = lax.axis_index("blk"), lax.axis_index("head"), lax.axis_index("batch")
    zl, y = blk // 4, blk % 4
    x, zh = head // 2, head % 2
    place = zh * 8 + zl
    clip = place % 2
    group = place // 2

    loads = [
        pltpu.make_async_copy(k_in, rows_in.at[0], l_sem.at[0]),
        pltpu.make_async_copy(v_in, sent.at[1], l_sem.at[1]),
        pltpu.make_async_copy(q_in, rows_in.at[1], l_sem.at[2]),
    ]
    for load in loads:
        load.start()

    def device(xx, yy, zz, cc):
        return {"blk": (zz % 8) * 4 + yy, "head": xx * 2 + zz // 8, "batch": cc}

    takers = [(2 * t + c, zh) for t in range(8)]
    holders = [(8 * c + s, clip) for s in range(8)]

    def is_me(d):
        return (d[0] == place) & (d[1] == c)

    def column(d):
        return device(x, y, d[0], d[1])

    def moved(first, second):
        dx = jnp.where(c == 0, first, second)
        dy = jnp.where(c == 0, second, first)
        return device((x + dx) % 4, (y + dy) % 4, place, c)

    near = [moved(1, 0), moved(3, 0), moved(0, 1), moved(0, 3)]
    partner = device(x, y, place, 1 - c)

    barrier = pltpu.get_barrier_semaphore()
    for d in takers + holders:
        @pl.when(jnp.logical_not(is_me(d)))
        def _(d=d):
            pl.semaphore_signal(barrier, inc=1, device_id=column(d), device_id_type=MESH)
    for d in near + [partner]:
        pl.semaphore_signal(barrier, inc=1, device_id=d, device_id_type=MESH)

    loads[0].wait()
    sent[0] = normalize(rows_in[0], kg[...])
    loads[1].wait()

    self_pair = (clip == c) & (zh == c)
    pl.semaphore_wait(barrier, 21 - 2 * self_pair.astype(jnp.int32))

    my_rows = pl.ds(pl.multiple_of(zl % 4 * 32, 32), 32)

    def a_dst(kind):
        if kind == 2:
            return q_all.at[pl.ds(pl.multiple_of(zl * 32, 32), 32), :]
        return mine.at[0, kind, zl // 4, my_rows, :]

    def a_src(kind, t):
        return sent.at[kind, :, t * COLS:(t + 1) * COLS]

    def a_copy(kind, t):
        return pltpu.make_async_remote_copy(
            src_ref=a_src(kind, t), dst_ref=a_dst(kind), send_sem=a_send.at[kind, t], recv_sem=a_recv.at[kind, zl],
            device_id=column(takers[t]), device_id_type=MESH,
        )

    def a_start(kind):
        for t in range(8):
            own = is_me(takers[t])

            @pl.when(jnp.logical_not(own))
            def _(t=t):
                a_copy(kind, t).start()

            @pl.when(own)
            def _(t=t):
                pltpu.make_async_copy(a_src(kind, t), a_dst(kind), a_recv.at[kind, zl]).start()

    a_start(0)
    a_start(1)
    loads[2].wait()
    sent[2] = normalize(rows_in[1], qg[...])
    a_start(2)

    tiles = mask.shape[0]
    q_tile = lax.broadcasted_iota(jnp.int32, (tiles, 256), 1) // 32 * 8 + y * 2 + x // 2
    pick = (lax.broadcasted_iota(jnp.int32, (tiles, 256), 0) == q_tile).astype(jnp.float32)
    live = lax.dot_general(
        mask[...].astype(jnp.float32), pick, (((0,), (0,)), ((), ())), preferred_element_type=jnp.float32
    )
    live = jnp.where(live > 0.5, 0.0, NEG)
    for i in range(8):
        bias[:, i, :] = live[i * 8:(i + 1) * 8, :]

    scale = HDIM ** (-0.5) * math.log2(math.e)
    run_max[...] = jnp.full(run_max.shape, 2.0 * NEG, jnp.float32)
    run_sum[...] = jnp.zeros(run_sum.shape, jnp.float32)
    acc[...] = jnp.zeros(acc.shape, jnp.float32)

    def await_rows(kind):
        for s in range(8):
            if kind == 2:
                dst = q_all.at[s * 32:(s + 1) * 32, :]
            else:
                dst = mine.at[0, kind, s // 4, s % 4 * 32:(s % 4 + 1) * 32, :]
            pltpu.make_async_copy(dst, dst, a_recv.at[kind, s]).wait()

    def hop(way, slot, to, kind, half):
        return pltpu.make_async_remote_copy(
            src_ref=mine.at[slot, kind, half], dst_ref=mine.at[to, kind, half],
            send_sem=r_send.at[way, slot, kind, half], recv_sem=r_recv.at[to, kind, half],
            device_id=near[way], device_id_type=MESH,
        )

    def across(slot, kind):
        return pltpu.make_async_remote_copy(
            src_ref=mine.at[slot, kind], dst_ref=theirs.at[slot, kind],
            send_sem=p_send.at[slot, kind], recv_sem=p_recv.at[slot, kind],
            device_id=partner, device_id_type=MESH,
        )

    def order(e):
        j = jnp.where(e < 4, e, (e - 4) // 3)
        a = jnp.where(j == 0, 0, jnp.where(j == 1, 3, j - 1))
        t = (e + 2) % 3
        b = jnp.where(e < 4, 0, jnp.where(t == 0, 3, t))
        return a, b

    def hops(e, kind, act):
        a, b = order(e)
        slot = a * 4 + b

        @pl.when(b == 0)
        def _():
            for half in range(2):
                act(hop(2, slot, a * 4 + 3, kind, half))
                act(hop(3, slot, a * 4 + 1, kind, half))

        @pl.when(b == 3)
        def _():
            act(hop(2, slot, a * 4 + 2, kind, 0))

        @pl.when(b == 1)
        def _():
            act(hop(3, slot, a * 4 + 2, kind, 1))

        @pl.when((b == 0) & (a == 3))
        def _():
            act(hop(0, slot, 8, kind, 0))

        @pl.when((b == 0) & (a == 1))
        def _():
            act(hop(1, slot, 8, kind, 1))

        act(across(slot, kind))

    def first_hops(kind, act):
        for half in range(2):
            act(hop(0, 0, 12, kind, half))
            act(hop(1, 0, 4, kind, half))
        hops(0, kind, act)

    def start(copy):
        copy.start()

    def wait_send(copy):
        copy.wait_send()

    def event(e, kind):
        a, b = order(e)
        slot = a * 4 + b
        for half in range(2):
            dst = mine.at[slot, kind, half]
            pltpu.make_async_copy(dst, dst, r_recv.at[slot, kind, half]).wait()
        hops(e, kind, start)

    def attend(held, slot, source_x, source_y):
        tile_bias = bias[source_y * 2 + source_x // 2]
        for h in range(GROUP):
            cols = slice(h * HDIM, (h + 1) * HDIM)
            keys = held[slot, 0, :, :, cols].reshape(256, HDIM)
            values = held[slot, 1, :, :, cols].reshape(256, HDIM)
            scores = lax.dot_general(
                keys, q_all[:, cols], (((1,), (1,)), ((), ())), preferred_element_type=jnp.float32
            )
            scores = scores.reshape(8, 32, 256) * scale + tile_bias[:, None, :]
            scores = scores.reshape(256, 256)
            old_max = run_max[h]
            new_max = jnp.maximum(old_max, jnp.max(scores, axis=0, keepdims=True))
            weights = jnp.exp2(scores - new_max)
            rescale = jnp.exp2(old_max - new_max)
            run_max[h] = new_max
            run_sum[h] = run_sum[h] * rescale + jnp.sum(weights, axis=0, keepdims=True)
            product = lax.dot_general(
                values, weights.astype(jnp.bfloat16), (((0,), (0,)), ((), ())), preferred_element_type=jnp.float32
            )
            acc[h] = acc[h] * rescale + product

    def both(e):
        a, b = order(e)
        slot = a * 4 + b
        dx, dy = jnp.where(c == 0, a, b), jnp.where(c == 0, b, a)
        attend(mine, slot, (x + dx) % 4, (y + dy) % 4)
        for kind in range(2):
            dst = theirs.at[slot, kind]
            pltpu.make_async_copy(dst, dst, p_recv.at[slot, kind]).wait()
        attend(theirs, slot, (x + dy) % 4, (y + dx) % 4)

    def loop(first, last, body):
        def step(e, carry):
            body(e)
            return carry

        lax.fori_loop(first, last, step, 0)

    await_rows(0)
    first_hops(0, start)
    loop(1, 11, lambda e: event(e, 0))
    await_rows(1)
    first_hops(1, start)
    loop(11, 16, lambda e: event(e, 0))
    loop(1, 4, lambda e: event(e, 1))
    await_rows(2)

    def turn(e):
        @pl.when((e >= 4) & (e < 16))
        def _():
            event(e, 1)

        lo = jnp.where(e < 7, 2 * (e - 4), e - 1)
        hi = jnp.where(e < 7, 2 * (e - 4) + 2, e)
        loop(lo, hi, both)

    loop(4, 17, turn)

    for h in range(GROUP):
        mixed[:, h * HDIM:(h + 1) * HDIM] = jnp.transpose(acc[h] / run_sum[h]).astype(jnp.bfloat16)

    def o_dst():
        return out.at[:, pl.ds(pl.multiple_of(group * COLS, 128), COLS)]

    def o_copy(s):
        return pltpu.make_async_remote_copy(
            src_ref=mixed.at[s * 32:(s + 1) * 32, :], dst_ref=o_dst(), send_sem=o_send.at[s], recv_sem=o_recv.at[group],
            device_id=column(holders[s]), device_id_type=MESH,
        )

    for s in range(8):
        own = is_me(holders[s])

        @pl.when(jnp.logical_not(own))
        def _(s=s):
            o_copy(s).start()

        @pl.when(own)
        def _(s=s):
            pltpu.make_async_copy(mixed.at[s * 32:(s + 1) * 32, :], o_dst(), o_recv.at[group]).start()

    for kind in range(3):
        for t in range(8):
            @pl.when(jnp.logical_not(is_me(takers[t])))
            def _(kind=kind, t=t):
                a_copy(kind, t).wait_send()
    for kind in range(2):
        first_hops(kind, wait_send)
        loop(1, 16, lambda e: hops(e, kind, wait_send))
    for s in range(8):
        @pl.when(jnp.logical_not(is_me(holders[s])))
        def _(s=s):
            o_copy(s).wait_send()
    for g in range(8):
        dst = out.at[:, g * COLS:(g + 1) * COLS]
        pltpu.make_async_copy(dst, dst, o_recv.at[g]).wait()


def per_device(query_rows, key_rows, value_rows, q_gain, k_gain, tile_mask):
    rows, width = query_rows.shape
    bf16, f32 = jnp.bfloat16, jnp.float32
    vmem = pl.BlockSpec(memory_space=pltpu.VMEM)
    hbm = pl.BlockSpec(memory_space=pl.ANY)
    dma = pltpu.SemaphoreType.DMA
    return pl.pallas_call(
        kernel,
        out_shape=jax.ShapeDtypeStruct((rows, width), bf16),
        in_specs=[hbm] * 3 + [vmem] * 3,
        out_specs=vmem,
        scratch_shapes=[
            pltpu.VMEM((2, rows, width), bf16),
            pltpu.VMEM((3, rows, width), bf16),
            pltpu.VMEM((16, 2, 2, 128, COLS), bf16),
            pltpu.VMEM((16, 2, 2, 128, COLS), bf16),
            pltpu.VMEM((256, COLS), bf16),
            pltpu.VMEM((8, 8, 256), f32),
            pltpu.VMEM((GROUP, 1, 256), f32),
            pltpu.VMEM((GROUP, 1, 256), f32),
            pltpu.VMEM((GROUP, HDIM, 256), f32),
            pltpu.VMEM((256, COLS), bf16),
            dma((3,)),
            dma((3, 8)), dma((3, 8)),
            dma((4, 16, 2, 2)), dma((16, 2, 2)),
            dma((16, 2)), dma((16, 2)),
            dma((8,)), dma((8,)),
        ],
        compiler_params=pltpu.CompilerParams(
            collective_id=0, has_side_effects=True, vmem_limit_bytes=62 * 1024 * 1024
        ),
    )(query_rows, key_rows, value_rows, q_gain.reshape(1, width), k_gain.reshape(1, width), tile_mask)


def solution(mesh):
    rows = P(("batch", "blk", "head"), None)
    return jax.shard_map(
        per_device,
        mesh=mesh,
        in_specs=(rows, rows, rows, P(), P(), P()),
        out_specs=rows,
        check_vma=False,
    )
```

time: 106 us -> 123 us (1.16)
  the two profiles are of different devices: /device:TPU:6 before, /device:TPU:65 now
where the time goes in v2:
time: 123 us
  Pallas kernels  121 us (98%)
  local copies, waits for them, and re-layouts  1.62 us (1%)
    pallas_call x1, Pallas kernels, per_device(): pl.pallas_call(kernel, out_shape=jax.ShapeDtypeStruct((rows, width), bf16...  121 us

profile of v2, /device:TPU:65, one launch (start us, length us, event | category | flops | bytes accessed | tf_op | source)
XLA Modules:
  0.0 122.9 jit_solution(17304859466543830713)
XLA Ops:
  0.0 121.3 %shard_map.64 = bf16[32,3072]{1,0:T(8,128)(2,1)} custom-call(bf16[32,3072]{1,0:T(8,128)(2,1)} %q_in.1, bf16[32,3072]{1,0:T(8,128)(2,1)} %k_in.1, bf16[32,3072]{1,0:T(8,128)(2,1)} %v_in.1, f32[1,3072]{1,0:T(1,128)} %bitcast.2, f32[1,3072]{1,0:T(1,128)} %bitcast.3, s32[64,64]{1,0:T(8,128)} %mask.1), custom_call_target="tpu_custom_call" | custom-call | tf_op jit(solution)/shard_map/pallas_call | solution.py:311
  121.3 1.6 %copy.8 = bf16[32,3072]{1,0:T(8,128)(2,1)} copy(bf16[32,3072]{1,0:T(8,128)(2,1)} %shard_map.64) | data formatting | bytes 393216

commit v3 on v2

--- a/solution.py
+++ b/solution.py
@@ -45,8 +45,11 @@
     def device(xx, yy, zz, cc):
         return {"blk": (zz % 8) * 4 + yy, "head": xx * 2 + zz // 8, "batch": cc}
 
-    takers = [(2 * t + c, zh) for t in range(8)]
-    holders = [(8 * c + s, clip) for s in range(8)]
+    far_first = (4, 3, 5, 2, 6, 1, 7, 0)
+    taker_groups = [(group + r) % 8 for r in far_first]
+    takers = [(2 * g + c, zh) for g in taker_groups]
+    holder_rows = [(zl + r) % 8 for r in far_first]
+    holders = [(8 * c + s, clip) for s in holder_rows]
 
     def is_me(d):
         return (d[0] == place) & (d[1] == c)
@@ -85,7 +88,7 @@
         return mine.at[0, kind, zl // 4, my_rows, :]
 
     def a_src(kind, t):
-        return sent.at[kind, :, t * COLS:(t + 1) * COLS]
+        return sent.at[kind, :, pl.ds(pl.multiple_of(taker_groups[t] * COLS, 128), COLS)]
 
     def a_copy(kind, t):
         return pltpu.make_async_remote_copy(
@@ -149,10 +152,9 @@
         )
 
     def order(e):
-        j = jnp.where(e < 4, e, (e - 4) // 3)
+        j = jnp.where(e < 4, e, jnp.where(e < 12, (e - 4) // 2, e - 12))
         a = jnp.where(j == 0, 0, jnp.where(j == 1, 3, j - 1))
-        t = (e + 2) % 3
-        b = jnp.where(e < 4, 0, jnp.where(t == 0, 3, t))
+        b = jnp.where(e < 4, 0, jnp.where(e < 12, 3 - e % 2 * 2, 2))
         return a, b
 
     def hops(e, kind, act):
@@ -203,37 +205,43 @@
             pltpu.make_async_copy(dst, dst, r_recv.at[slot, kind, half]).wait()
         hops(e, kind, start)
 
-    def attend(held, slot, source_x, source_y):
-        tile_bias = bias[source_y * 2 + source_x // 2]
+    def attend(slot, tile_bias):
         for h in range(GROUP):
             cols = slice(h * HDIM, (h + 1) * HDIM)
-            keys = held[slot, 0, :, :, cols].reshape(256, HDIM)
-            values = held[slot, 1, :, :, cols].reshape(256, HDIM)
-            scores = lax.dot_general(
-                keys, q_all[:, cols], (((1,), (1,)), ((), ())), preferred_element_type=jnp.float32
-            )
-            scores = scores.reshape(8, 32, 256) * scale + tile_bias[:, None, :]
-            scores = scores.reshape(256, 256)
             old_max = run_max[h]
-            new_max = jnp.maximum(old_max, jnp.max(scores, axis=0, keepdims=True))
-            weights = jnp.exp2(scores - new_max)
+            new_max, scores = old_max, []
+            for held, held_bias in zip((mine, theirs), tile_bias):
+                score = lax.dot_general(
+                    held[slot, 0, :, :, cols].reshape(256, HDIM), q_all[:, cols], (((1,), (1,)), ((), ())),
+                    preferred_element_type=jnp.float32,
+                )
+                score = (score.reshape(8, 32, 256) * scale + held_bias[:, None, :]).reshape(256, 256)
+                new_max = jnp.maximum(new_max, jnp.max(score, axis=0, keepdims=True))
+                scores.append(score)
             rescale = jnp.exp2(old_max - new_max)
+            total, product = run_sum[h] * rescale, acc[h] * rescale
+            for held, score in zip((mine, theirs), scores):
+                weights = jnp.exp2(score - new_max)
+                total = total + jnp.sum(weights, axis=0, keepdims=True)
+                product = product + lax.dot_general(
+                    held[slot, 1, :, :, cols].reshape(256, HDIM), weights.astype(jnp.bfloat16),
+                    (((0,), (0,)), ((), ())), preferred_element_type=jnp.float32,
+                )
             run_max[h] = new_max
-            run_sum[h] = run_sum[h] * rescale + jnp.sum(weights, axis=0, keepdims=True)
-            product = lax.dot_general(
-                values, weights.astype(jnp.bfloat16), (((0,), (0,)), ((), ())), preferred_element_type=jnp.float32
-            )
-            acc[h] = acc[h] * rescale + product
+            run_sum[h] = total
+            acc[h] = product
 
     def both(e):
         a, b = order(e)
         slot = a * 4 + b
         dx, dy = jnp.where(c == 0, a, b), jnp.where(c == 0, b, a)
-        attend(mine, slot, (x + dx) % 4, (y + dy) % 4)
         for kind in range(2):
             dst = theirs.at[slot, kind]
             pltpu.make_async_copy(dst, dst, p_recv.at[slot, kind]).wait()
-        attend(theirs, slot, (x + dy) % 4, (y + dx) % 4)
+        attend(slot, (
+            bias[(y + dy) % 4 * 2 + (x + dx) % 4 // 2],
+            bias[(y + dx) % 4 * 2 + (x + dy) % 4 // 2],
+        ))
 
     def loop(first, last, body):
         def step(e, carry):
@@ -244,23 +252,27 @@
 
     await_rows(0)
     first_hops(0, start)
-    loop(1, 11, lambda e: event(e, 0))
+    loop(1, 8, lambda e: event(e, 0))
     await_rows(1)
     first_hops(1, start)
-    loop(11, 16, lambda e: event(e, 0))
+    loop(8, 12, lambda e: event(e, 0))
     loop(1, 4, lambda e: event(e, 1))
     await_rows(2)
 
-    def turn(e):
-        @pl.when((e >= 4) & (e < 16))
-        def _():
-            event(e, 1)
-
-        lo = jnp.where(e < 7, 2 * (e - 4), e - 1)
-        hi = jnp.where(e < 7, 2 * (e - 4) + 2, e)
-        loop(lo, hi, both)
-
-    loop(4, 17, turn)
+    def late_keys(e):
+        event(e, 0)
+        both(e - 12)
+
+    def late_values(e):
+        event(e, 1)
+
+        @pl.when(e > 4)
+        def _():
+            both(e - 1)
+
+    loop(12, 16, late_keys)
+    loop(4, 16, late_values)
+    both(15)
 
     for h in range(GROUP):
         mixed[:, h * HDIM:(h + 1) * HDIM] = jnp.transpose(acc[h] / run_sum[h]).astype(jnp.bfloat16)
@@ -268,9 +280,12 @@
     def o_dst():
         return out.at[:, pl.ds(pl.multiple_of(group * COLS, 128), COLS)]
 
+    def o_src(s):
+        return mixed.at[pl.ds(pl.multiple_of(holder_rows[s] * 32, 32), 32), :]
+
     def o_copy(s):
         return pltpu.make_async_remote_copy(
-            src_ref=mixed.at[s * 32:(s + 1) * 32, :], dst_ref=o_dst(), send_sem=o_send.at[s], recv_sem=o_recv.at[group],
+            src_ref=o_src(s), dst_ref=o_dst(), send_sem=o_send.at[s], recv_sem=o_recv.at[group],
             device_id=column(holders[s]), device_id_type=MESH,
         )
 
@@ -283,7 +298,7 @@
 
         @pl.when(own)
         def _(s=s):
-            pltpu.make_async_copy(mixed.at[s * 32:(s + 1) * 32, :], o_dst(), o_recv.at[group]).start()
+            pltpu.make_async_copy(o_src(s), o_dst(), o_recv.at[group]).start()
 
     for kind in range(3):
         for t in range(8):

time: 123 us -> 94.3 us (0.77)
  the two profiles are of different devices: /device:TPU:65 before, /device:TPU:6 now
where the time goes in v3:
time: 94.3 us; the launch traced here: 92.9 us
  Pallas kernels  91.2 us (97%)
  local copies, waits for them, and re-layouts  1.62 us (2%)
    pallas_call x1, Pallas kernels, per_device(): pl.pallas_call(kernel, out_shape=jax.ShapeDtypeStruct((rows, width), bf16...  91.2 us

profile of v3, /device:TPU:6, one launch (start us, length us, event | category | flops | bytes accessed | tf_op | source)
XLA Modules:
  0.0 92.9 jit_solution(15239346915405169012)
XLA Ops:
  0.0 91.2 %shard_map.64 = bf16[32,3072]{1,0:T(8,128)(2,1)} custom-call(bf16[32,3072]{1,0:T(8,128)(2,1)} %q_in.1, bf16[32,3072]{1,0:T(8,128)(2,1)} %k_in.1, bf16[32,3072]{1,0:T(8,128)(2,1)} %v_in.1, f32[1,3072]{1,0:T(1,128)} %bitcast.2, f32[1,3072]{1,0:T(1,128)} %bitcast.3, s32[64,64]{1,0:T(8,128)} %mask.1), custom_call_target="tpu_custom_call" | custom-call | tf_op jit(solution)/shard_map/pallas_call | solution.py:326
  91.2 1.6 %copy.8 = bf16[32,3072]{1,0:T(8,128)(2,1)} copy(bf16[32,3072]{1,0:T(8,128)(2,1)} %shard_map.64) | data formatting | bytes 393216

commit v4 on v3

--- a/solution.py
+++ b/solution.py
@@ -252,10 +252,10 @@
 
     await_rows(0)
     first_hops(0, start)
-    loop(1, 8, lambda e: event(e, 0))
+    loop(1, 4, lambda e: event(e, 0))
     await_rows(1)
     first_hops(1, start)
-    loop(8, 12, lambda e: event(e, 0))
+    loop(4, 12, lambda e: event(e, 0))
     loop(1, 4, lambda e: event(e, 1))
     await_rows(2)
 

time: 94.3 us -> 93.6 us (level)
  the two profiles are of different devices: /device:TPU:6 before, /device:TPU:32 now
where the time goes in v4:
time: 93.6 us; the launch traced here: 93.4 us
  Pallas kernels  91.8 us (98%)
  local copies, waits for them, and re-layouts  1.62 us (2%)
    pallas_call x1, Pallas kernels, per_device(): pl.pallas_call(kernel, out_shape=jax.ShapeDtypeStruct((rows, width), bf16...  91.8 us

profile of v4, /device:TPU:32, one launch (start us, length us, event | category | flops | bytes accessed | tf_op | source)
XLA Modules:
  0.0 93.4 jit_solution(9685523369048479213)
XLA Ops:
  0.0 91.8 %shard_map.64 = bf16[32,3072]{1,0:T(8,128)(2,1)} custom-call(bf16[32,3072]{1,0:T(8,128)(2,1)} %q_in.1, bf16[32,3072]{1,0:T(8,128)(2,1)} %k_in.1, bf16[32,3072]{1,0:T(8,128)(2,1)} %v_in.1, f32[1,3072]{1,0:T(1,128)} %bitcast.2, f32[1,3072]{1,0:T(1,128)} %bitcast.3, s32[64,64]{1,0:T(8,128)} %mask.1), custom_call_target="tpu_custom_call" | custom-call | tf_op jit(solution)/shard_map/pallas_call | solution.py:326
  91.8 1.6 %copy.8 = bf16[32,3072]{1,0:T(8,128)(2,1)} copy(bf16[32,3072]{1,0:T(8,128)(2,1)} %shard_map.64) | data formatting | bytes 393216
